TPU v7x, 32 devices: a whole 2x2x4 slice. The times are simulated.
32 devices in a mesh: leaf: 8 (over y, x, core), seq: 4 (over z).
Axes of the slice: x: 2, y: 2, z: 4, core: 2. Of those that a mesh axis runs over, the one named last changes fastest.
Arguments:
- prompt_q: bfloat16 [8, 512, 1792], P('leaf', 'seq'), may hold values from -6 to 6
- prompt_k: bfloat16 [8, 512, 256], P('leaf', 'seq'), may hold values from -6 to 6
- prompt_value_rows: bfloat16 [8, 512, 256], P('leaf', 'seq'), may hold values from -6 to 6
- leaf_q: bfloat16 [8, 192, 1792], P('leaf', 'seq'), may hold values from -6 to 6
- leaf_k: bfloat16 [8, 192, 256], P('leaf', 'seq'), may hold values from -6 to 6
- leaf_value_rows: bfloat16 [8, 192, 256], P('leaf', 'seq'), may hold values from -6 to 6
- prompt_dy: bfloat16 [8, 512, 3584], P('leaf', 'seq'), may hold values from -6 to 6
- leaf_dy: bfloat16 [8, 192, 3584], P('leaf', 'seq'), may hold values from -6 to 6
- out_weight: bfloat16 [1792, 3584], replicated, may hold values from -0.125 to 0.125
- lengths: int32 [8, 16], P('leaf'), may hold values from 1 to 24, 192 in all within a row
- offsets: int32 [8, 16], P('leaf'), may hold values from 1 to 512
- parents: int32 [8, 16], P('leaf'), may hold values from 0 to 15, as said below
Outputs:
- prompt_dq: float32 [8, 512, 1792], P('leaf', 'seq')
- prompt_dk: float32 [8, 512, 256], P('leaf', 'seq')
- prompt_dv: float32 [8, 512, 256], P('leaf', 'seq')
- leaf_dq: float32 [8, 192, 1792], P('leaf', 'seq')
- leaf_dk: float32 [8, 192, 256], P('leaf', 'seq')
- leaf_dv: float32 [8, 192, 256], P('leaf', 'seq')
- weight_grad: float32 [1792, 3584], P(('leaf', 'seq'))
Inputs may be any that keep to these rules, and one draw needn't show every extreme that they name: parents[t, b] lies in 0 to b; the value b means that branch b has no ancestor branch.
All inputs are finite; a program needn't handle non-finite values.
Results may differ from a plain program's by a relative error of at most 0.025.
Values may be sent and summed in bfloat16 or wider, within the bound.
No kernel may reach another device: no remote copies, remote signals or barrier semaphores. Data moves between devices by JAX's collectives and lax.ppermute only.
A program may use at most 128 MiB of HBM per device.

v0:
```python
import math
import jax
import jax.numpy as jnp
from jax import lax
from jax.sharding import PartitionSpec as P

HEAD_SIZE = 128
QUERY_HEADS = 14
KEY_VALUE_HEADS = 2
QUERY_PER_KV = 7


def leaf_visibility(lengths, offsets, parents, query_index, prompt_total, leaf_total):
    branch_ends = jnp.cumsum(lengths)
    branch_ids = jnp.arange(lengths.shape[0], dtype=jnp.int32)
    leaf_index = jnp.arange(leaf_total, dtype=jnp.int32)
    key_branch = jnp.sum((leaf_index[:, None] >= branch_ends[None, :]).astype(jnp.int32), axis=1)
    query_branch = jnp.sum((query_index[:, None] >= branch_ends[None, :]).astype(jnp.int32), axis=1)
    member = (query_branch[:, None] == branch_ids[None, :]).astype(jnp.int32)
    fork_point = jnp.sum(member * offsets[None, :], axis=1)
    ancestor = jnp.sum(member * parents[None, :], axis=1)
    prompt_index = jnp.arange(prompt_total, dtype=jnp.int32)
    sees_prompt = prompt_index[None, :] < fork_point[:, None]
    own_branch = (key_branch[None, :] == query_branch[:, None]) & (
        leaf_index[None, :] <= query_index[:, None]
    )
    inherited = (key_branch[None, :] == ancestor[:, None]) & (
        ancestor[:, None] != query_branch[:, None]
    )
    return jnp.concatenate([sees_prompt, own_branch | inherited], axis=1)


def weight_gradient(attn_out, upstream, tree_count, seq_count):
    width_total = attn_out.shape[1]
    device_rows = attn_out.shape[0]
    row_share = width_total // (tree_count * seq_count)
    normalizer = 1.0 / math.sqrt(tree_count * seq_count * device_rows)
    parted = attn_out.reshape(device_rows, tree_count, seq_count, row_share)
    moved = lax.all_to_all(parted, "seq", split_axis=2, concat_axis=0, tiled=True)
    picked = moved.reshape(device_rows * seq_count, tree_count * row_share)
    tree_grad = lax.all_gather(upstream, "seq", axis=0, tiled=True)
    partial_term = lax.dot_general(
        picked, tree_grad, (((0,), (0,)), ((), ())), preferred_element_type=jnp.float32
    )
    summed = lax.psum_scatter(
        partial_term.astype(jnp.bfloat16), "leaf", scatter_dimension=0, tiled=True
    ).astype(jnp.float32)
    return summed * normalizer


def body(
    prompt_q,
    prompt_k,
    prompt_value_rows,
    leaf_q,
    leaf_k,
    leaf_value_rows,
    prompt_dy,
    leaf_dy,
    out_weight,
    lengths,
    offsets,
    parents,
):
    seq_count = lax.axis_size("seq")
    tree_count = lax.axis_size("leaf")
    seq_index = lax.axis_index("seq")
    prompt_dev = prompt_q.shape[1]
    leaf_dev = leaf_q.shape[1]
    device_rows = prompt_dev + leaf_dev
    prompt_total = prompt_dev * seq_count
    leaf_total = leaf_dev * seq_count
    score_scale = 1.0 / math.sqrt(HEAD_SIZE)
    gathered = (
        lax.all_gather(prompt_k, "seq", axis=1, tiled=True),
        lax.all_gather(prompt_value_rows, "seq", axis=1, tiled=True),
        lax.all_gather(leaf_k, "seq", axis=1, tiled=True),
        lax.all_gather(leaf_value_rows, "seq", axis=1, tiled=True),
    )
    key_rows = jnp.concatenate([gathered[0][0], gathered[2][0]], axis=0)
    value_rows = jnp.concatenate([gathered[1][0], gathered[3][0]], axis=0)
    query_rows = jnp.concatenate([prompt_q[0], leaf_q[0]], axis=0)
    upstream = jnp.concatenate([prompt_dy[0], leaf_dy[0]], axis=0)
    prompt_index = seq_index * prompt_dev + jnp.arange(prompt_dev, dtype=jnp.int32)
    leaf_index = seq_index * leaf_dev + jnp.arange(leaf_dev, dtype=jnp.int32)
    prompt_keys = jnp.arange(prompt_total, dtype=jnp.int32)
    prompt_sees = jnp.concatenate(
        [
            prompt_keys[None, :] <= prompt_index[:, None],
            jnp.zeros((prompt_dev, leaf_total), dtype=jnp.bool_),
        ],
        axis=1,
    )
    leaf_sees = leaf_visibility(
        lengths[0], offsets[0], parents[0], leaf_index, prompt_total, leaf_total
    )
    visible = jnp.concatenate([prompt_sees, leaf_sees], axis=0)
    grouped_queries = query_rows.reshape(device_rows, KEY_VALUE_HEADS, QUERY_PER_KV, HEAD_SIZE)
    output_gradient = lax.dot_general(
        upstream, out_weight, (((1,), (1,)), ((), ())), preferred_element_type=jnp.float32
    ).astype(jnp.bfloat16)
    gradient_groups = output_gradient.reshape(device_rows, KEY_VALUE_HEADS, QUERY_PER_KV, HEAD_SIZE)
    prob_list, weight_list, attn_list = ([], [], [])
    for key_value_group in range(KEY_VALUE_HEADS):
        key_block = key_rows[:, key_value_group * HEAD_SIZE : (key_value_group + 1) * HEAD_SIZE]
        value_block = value_rows[:, key_value_group * HEAD_SIZE : (key_value_group + 1) * HEAD_SIZE]
        scores = (
            jnp.einsum(
                "qhd,kd->hqk",
                grouped_queries[:, key_value_group],
                key_block,
                preferred_element_type=jnp.float32,
            )
            * score_scale
        )
        scores = jnp.where(visible[None], scores, -jnp.inf)
        shifted = jnp.exp(scores - jnp.max(scores, axis=2, keepdims=True))
        probabilities = shifted / jnp.sum(shifted, axis=2, keepdims=True)
        weights = probabilities.astype(jnp.bfloat16)
        attn_list.append(
            jnp.einsum(
                "hqk,kd->qhd", weights, value_block, preferred_element_type=jnp.float32
            ).astype(jnp.bfloat16)
        )
        prob_list.append(probabilities)
        weight_list.append(weights)
    attn_out = jnp.stack(attn_list, axis=1).reshape(device_rows, QUERY_HEADS * HEAD_SIZE)
    dscore_list, dq_list = ([], [])
    for key_value_group in range(KEY_VALUE_HEADS):
        key_block = key_rows[:, key_value_group * HEAD_SIZE : (key_value_group + 1) * HEAD_SIZE]
        value_block = value_rows[:, key_value_group * HEAD_SIZE : (key_value_group + 1) * HEAD_SIZE]
        row_dot = jnp.sum(
            gradient_groups[:, key_value_group].astype(jnp.float32)
            * attn_list[key_value_group].astype(jnp.float32),
            axis=2,
        )
        prob_grad = jnp.einsum(
            "qhd,kd->hqk",
            gradient_groups[:, key_value_group],
            value_block,
            preferred_element_type=jnp.float32,
        )
        dscore = (
            prob_list[key_value_group] * (prob_grad - row_dot.T[:, :, None]) * score_scale
        ).astype(jnp.bfloat16)
        dq_list.append(
            jnp.einsum("hqk,kd->qhd", dscore, key_block, preferred_element_type=jnp.float32)
        )
        dscore_list.append(dscore)
    query_grad = jnp.stack(dq_list, axis=1).reshape(device_rows, QUERY_HEADS * HEAD_SIZE)
    first_block = jnp.int32(0) // device_rows
    blocks = device_rows * lax.axis_size("seq") // device_rows
    prompt_cols = blocks * prompt_dev
    leaf_cols = blocks * leaf_dev
    key_parts = []
    value_parts = []
    for key_value_group in range(KEY_VALUE_HEADS):
        picked_d = jnp.concatenate(
            [
                lax.dynamic_slice_in_dim(
                    dscore_list[key_value_group], first_block * prompt_dev, prompt_cols, 2
                ),
                lax.dynamic_slice_in_dim(dscore_list[key_value_group], prompt_total, leaf_cols, 2),
            ],
            axis=2,
        )
        picked_w = jnp.concatenate(
            [
                lax.dynamic_slice_in_dim(
                    weight_list[key_value_group], first_block * prompt_dev, prompt_cols, 2
                ),
                lax.dynamic_slice_in_dim(weight_list[key_value_group], prompt_total, leaf_cols, 2),
            ],
            axis=2,
        )
        key_parts.append(
            jnp.einsum(
                "hqk,qhd->kd",
                picked_d,
                grouped_queries[:, key_value_group],
                preferred_element_type=jnp.float32,
            )
        )
        value_parts.append(
            jnp.einsum(
                "hqk,qhd->kd",
                picked_w,
                gradient_groups[:, key_value_group],
                preferred_element_type=jnp.float32,
            )
        )
    joined = jnp.concatenate(key_parts + value_parts, axis=1)
    stacked_width = joined.shape[1]
    prompt_part = joined[:prompt_cols].reshape(blocks, prompt_dev, stacked_width)
    leaf_part = joined[prompt_cols:].reshape(blocks, leaf_dev, stacked_width)
    key_grads = lax.psum_scatter(
        jnp.concatenate([prompt_part, leaf_part], axis=1)
        .reshape(device_rows * lax.axis_size("seq"), stacked_width)
        .astype(jnp.bfloat16),
        "seq",
        scatter_dimension=0,
        tiled=True,
    ).astype(jnp.float32)
    weight_grad = weight_gradient(attn_out, upstream, tree_count, seq_count)
    key_value_width = KEY_VALUE_HEADS * HEAD_SIZE
    return (
        query_grad[:prompt_dev][None],
        key_grads[:prompt_dev, :key_value_width][None],
        key_grads[:prompt_dev, key_value_width:][None],
        query_grad[prompt_dev:][None],
        key_grads[prompt_dev:, :key_value_width][None],
        key_grads[prompt_dev:, key_value_width:][None],
        weight_grad,
    )


def solution(mesh):
    placed = (
        P("leaf", "seq", None),
        P("leaf", "seq", None),
        P("leaf", "seq", None),
        P("leaf", "seq", None),
        P("leaf", "seq", None),
        P("leaf", "seq", None),
        P("leaf", "seq", None),
        P("leaf", "seq", None),
        P(),
        P("leaf", None),
        P("leaf", None),
        P("leaf", None),
    )
    return jax.shard_map(
        body,
        mesh=mesh,
        in_specs=placed,
        out_specs=(
            P("leaf", "seq", None),
            P("leaf", "seq", None),
            P("leaf", "seq", None),
            P("leaf", "seq", None),
            P("leaf", "seq", None),
            P("leaf", "seq", None),
            P(("leaf", "seq"), None),
        ),
        check_vma=False,
    )
```

profile of v0, /device:TPU:0, one launch (start us, length us, event | category | flops | bytes accessed | tf_op | source)
XLA Modules:
  0.0 209.9 jit_solution(18198870469097177820)
XLA Ops:
  7.3 2.5 %pad_maximum_fusion = bf16[176,3584]{1,0:T(8,128)(2,1)} fusion(bf16[48,3584]{1,0:T(8,128)(2,1)} %bitcast.198, bf16[128,3584]{1,0:T(8,128)(2,1)} %bitcast.187), kind=kLoop, calls=%fused_computation.31 | loop fusion | flops 2523136 | bytes 2523136 | tf_op jit(solution)/shard_map/concatenate | solution.py:83
  11.8 9.1 %convolution_convert_fusion.1 = bf16[176,1792]{1,0:T(8,128)(2,1)S(1)} fusion(bf16[1792,3584]{1,0:T(8,128)(2,1)} %param.20, bf16[48,3584]{1,0:T(8,128)(2,1)S(1)} %bitcast.199, bf16[128,3584]{1,0:T(8,128)(2,1)S(1)} %bitcast.188), kind=kOutput, calls=%fused_computation.17 | convolution fusion | flops 2263568384 | bytes 14737408 | tf_op jit(solution)/shard_map/dot_general | solution.py:99
  20.9 0.7 reshape.92
  21.7 16.0 %all_gather.16 = bf16[1,192,256]{2,1,0:T(8,128)(2,1)S(1)} all-gather(bf16[1,48,256]{2,1,0:T(8,128)(2,1)S(1)} %copy-done.27), channel_id=1, replica_groups=mesh['leaf'=8,'seq'=4] {'seq'}, dimensions={1}, use_global_device_ids=true | all-gather | bytes 122880 | tf_op jit(solution)/shard_map/all_gather | solution.py:77
  37.6 15.0 %all_gather.18 = bf16[1,192,256]{2,1,0:T(8,128)(2,1)S(1)} all-gather(bf16[1,48,256]{2,1,0:T(8,128)(2,1)S(1)} %copy-done.28), channel_id=1, replica_groups=mesh['leaf'=8,'seq'=4] {'seq'}, dimensions={1}, use_global_device_ids=true | all-gather | bytes 122880 | tf_op jit(solution)/shard_map/all_gather | solution.py:78
  52.7 18.1 %all_gather.15 = bf16[1,512,256]{2,1,0:T(8,128)(2,1)S(1)} all-gather(bf16[1,128,256]{2,1,0:T(8,128)(2,1)S(1)} %copy-done.26), channel_id=1, replica_groups=mesh['leaf'=8,'seq'=4] {'seq'}, dimensions={1}, use_global_device_ids=true | all-gather | bytes 327680 | tf_op jit(solution)/shard_map/all_gather | solution.py:75
  70.7 17.5 %all_gather.17 = bf16[1,512,256]{2,1,0:T(8,128)(2,1)S(1)} all-gather(bf16[1,128,256]{2,1,0:T(8,128)(2,1)} %param.14), channel_id=1, replica_groups=mesh['leaf'=8,'seq'=4] {'seq'}, dimensions={1}, use_global_device_ids=true | all-gather | bytes 327680 | tf_op jit(solution)/shard_map/all_gather | solution.py:76
  88.7 0.9 fusion.66
  89.6 3.3 %fusion.76 = (f32[7,176]{1,0:T(8,128)S(1)}, f32[7,176,704]{2,1,0:T(8,128)}) fusion(pred[176,704]{1,0:T(8,128)(4,1)S(1)} %pad_add_fusion, bf16[192,256]{1,0:T(8,128)(2,1)S(1)} %bitcast.189, bf16[512,256]{1,0:T(8,128)(2,1)S(1)} %bitcast.175, bf16[48,2,7,128]{3,0,2,1:T(8,128)(2,1)S(1)} %copy-done.24, bf16[128,2,7,128]{3,0,2,1:T(8,128)(2,1)S(1)} %copy.47), kind=kOutput, calls=%fused_computation.98 | convolution fusion | flops 226497216 | bytes 4589376 | tf_op jit(solution)/shard_map/sub | solution.py:117
  93.0 2.4 %fusion.17 = bf16[7,176,704]{2,1,0:T(8,128)(2,1)S(1)} fusion(f32[7,176,704]{2,1,0:T(8,128)} %get-tuple-element.41, f32[7,176]{1,0:T(8,128)S(1)} %get-tuple-element.40), kind=kLoop, calls=%fused_computation.27 | loop fusion | flops 1734656 | bytes 5208896 | tf_op jit(solution)/shard_map/convert_element_type | solution.py:119
  95.4 1.4 multiply_reduce_fusion
  96.8 4.3 %fusion.67 = (f32[7,176]{1,0:T(8,128)S(1)}, f32[7,176,704]{2,1,0:T(8,128)}) fusion(pred[176,704]{1,0:T(8,128)(4,1)S(1)} %pad_add_fusion, bf16[512,256]{1,0:T(8,128)(2,1)S(1)} %bitcast.176, bf16[192,256]{1,0:T(8,128)(2,1)S(1)} %bitcast.190, bf16[128,2,7,128]{3,0,2,1:T(8,128)(2,1)S(1)} %copy-done.20, bf16[48,2,7,128]{3,0,2,1:T(8,128)(2,1)} %copy.48), kind=kOutput, calls=%fused_computation.97 | convolution fusion | flops 226497216 | bytes 4589376 | tf_op jit(solution)/shard_map/sub | solution.py:117
  101.1 2.4 %fusion.16 = bf16[7,176,704]{2,1,0:T(8,128)(2,1)S(1)} fusion(f32[7,176,704]{2,1,0:T(8,128)} %get-tuple-element.37, f32[7,176]{1,0:T(8,128)S(1)} %get-tuple-element.36), kind=kLoop, calls=%fused_computation.26 | loop fusion | flops 1734656 | bytes 5208896 | tf_op jit(solution)/shard_map/convert_element_type | solution.py:119
  103.6 1.2 copy-done
  104.8 1.4 multiply_reduce_fusion.1
  106.7 1.0 copy.54
  107.7 5.6 %all-to-all-start = ((bf16[176,8,4,56]{0,3,1,2:T(8,128)(2,1)}), bf16[176,8,4,56]{0,3,1,2:T(8,128)(2,1)S(1)}, u32[]{:S(2)}, u32[]{:S(2)}) async-start(bf16[176,8,4,56]{0,3,1,2:T(8,128)(2,1)} %copy.54), calls=%async_computation.1 | async-start | bytes 1835008 | tf_op jit(solution)/shard_map/all_to_all | solution.py:39
  113.3 2.7 %fusion.4 = bf16[7,176,704]{2,1,0:T(8,128)(2,1)S(1)} fusion(f32[7,176]{1,0:T(8,128)S(1)} %bitcast.201, f32[7,176,704]{2,1,0:T(8,128)} %get-tuple-element.41, f32[7,176]{1,0:T(8,128)S(1)} %get-tuple-element.40, bf16[176,1,7,128]{3,2,1,0:T(8,128)(2,1)S(1)} %copy-done.14, bf16[192,256]{1,0:T(8,128)(2,1)} %bitcast.195, bf16[512,256]{1,0:T(8,128)(2,1)S(1)} %bitcast.181), kind=kOutput, calls=%fused_computation.6 | convolution fusion | flops 226733056 | bytes 5889664 | tf_op jit(solution)/shard_map/qhd,kd->hqk/dot_general | solution.py:137
  116.0 1.3 copy-done.7
  120.3 1.1 fusion.7
  121.4 0.7 convolution_bitcast_fusion.5
  122.7 0.9 pad_maximum_fusion.1
  123.7 22.3 %all-to-all-done = bf16[176,8,4,56]{0,3,1,2:T(8,128)(2,1)S(1)} async-done(((bf16[176,8,4,56]{0,3,1,2:T(8,128)(2,1)}), bf16[176,8,4,56]{0,3,1,2:T(8,128)(2,1)S(1)}, u32[]{:S(2)}, u32[]{:S(2)}) %all-to-all-start) | async-done | bytes 630816 | tf_op jit(solution)/shard_map/all_to_all | solution.py:39
  146.7 0.7 reshape.95
  147.5 6.5 %convolution_convert_fusion = bf16[448,3584]{1,0:T(8,128)(2,1)} fusion(bf16[704,448]{0,1:T(8,128)(2,1)S(1)} %reshape.95, bf16[704,3584]{1,0:T(8,128)(2,1)} %all-gather.2.cloned.1.call-done), kind=kOutput, calls=%fused_computation.2 | convolution fusion | flops 2262335488 | bytes 8888320 | tf_op jit(solution)/shard_map/dot_general | solution.py:42
  154.0 0.9 copy-done.4
  156.3 0.9 copy-done.10
  158.2 1.2 copy.56
  159.6 0.8 broadcast_in_dim.33
  160.4 0.9 convert_element_type.75
  162.7 38.7 %reduce-scatter.5.cloned.1.call-done = bf16[56,3584]{1,0:T(8,128)(2,1)} async-done(((bf16[448,3584]{1,0:T(8,128)(2,1)}), bf16[56,3584]{1,0:T(8,128)(2,1)}) %reduce-scatter.5.cloned.1.call-update) | async-done | bytes 401424 | tf_op jit(solution)/shard_map/reduce_scatter | solution.py:45
  201.5 1.9 convert_multiply_fusion
  (106 shorter events, 11.0 us)
Async XLA Ops:
  7.2 2.6 %copy-start.31 = (s32[1,16]{1,0:T(1,128)S(1)}, s32[1,16]{1,0:T(1,128)}, u32[]{:S(2)}) copy-start(s32[1,16]{1,0:T(1,128)} %param.21) | copy-start | bytes 196
  7.2 3.0 %copy-start.33 = (s32[1,16]{1,0:T(1,128)S(1)}, s32[1,16]{1,0:T(1,128)}, u32[]{:S(2)}) copy-start(s32[1,16]{1,0:T(1,128)} %param.23) | copy-start | bytes 196
  7.2 3.0 %copy-start.32 = (s32[1,16]{1,0:T(1,128)S(1)}, s32[1,16]{1,0:T(1,128)}, u32[]{:S(2)}) copy-start(s32[1,16]{1,0:T(1,128)} %param.22) | copy-start | bytes 196
  7.2 3.1 %copy-start.23 = (bf16[1,48,1792]{2,1,0:T(8,128)(2,1)S(1)}, bf16[1,48,1792]{2,1,0:T(8,128)(2,1)}, u32[]{:S(2)}) copy-start(bf16[1,48,1792]{2,1,0:T(8,128)(2,1)} %param.15) | copy-start | bytes 516100
  7.2 4.0 %copy-start.18 = (bf16[1,128,1792]{2,1,0:T(8,128)(2,1)S(1)}, bf16[1,128,1792]{2,1,0:T(8,128)(2,1)}, u32[]{:S(2)}) copy-start(bf16[1,128,1792]{2,1,0:T(8,128)(2,1)} %param.12) | copy-start | bytes 1376260
  7.2 140.3 %all-gather.2.cloned.1.call-start = ((), (), s32[]{:S(2)}) async-start(), calls=%async_computation.4 | async-start | bytes 6307840 | tf_op jit(solution)/shard_map/all_gather | solution.py:41
  9.8 2.0 copy-start.15
  9.8 2.0 copy-start.22
  11.7 77.9 %copy-start.19 = (bf16[128,2,7,128]{3,0,2,1:T(8,128)(2,1)}, bf16[128,2,7,128]{3,0,2,1:T(8,128)(2,1)S(1)}, u32[]{:S(2)}) copy-start(bf16[128,2,7,128]{3,0,2,1:T(8,128)(2,1)S(1)} %copy.47) | copy-start | bytes 1376260
  11.8 9.9 %copy-start.27 = (bf16[1,48,256]{2,1,0:T(8,128)(2,1)S(1)}, bf16[1,48,256]{2,1,0:T(8,128)(2,1)}, u32[]{:S(2)}) copy-start(bf16[1,48,256]{2,1,0:T(8,128)(2,1)} %param.16) | copy-start | bytes 73732
  11.8 25.9 %copy-start.28 = (bf16[1,48,256]{2,1,0:T(8,128)(2,1)S(1)}, bf16[1,48,256]{2,1,0:T(8,128)(2,1)}, u32[]{:S(2)}) copy-start(bf16[1,48,256]{2,1,0:T(8,128)(2,1)} %param.17) | copy-start | bytes 73732
  11.8 40.9 %copy-start.26 = (bf16[1,128,256]{2,1,0:T(8,128)(2,1)S(1)}, bf16[1,128,256]{2,1,0:T(8,128)(2,1)}, u32[]{:S(2)}) copy-start(bf16[1,128,256]{2,1,0:T(8,128)(2,1)} %param.13) | copy-start | bytes 196612
  20.9 68.7 %copy-start.24 = (bf16[48,2,7,128]{3,0,2,1:T(8,128)(2,1)S(1)}, bf16[48,2,7,128]{3,0,2,1:T(8,128)(2,1)}, u32[]{:S(2)}) copy-start(bf16[48,2,7,128]{3,0,2,1:T(8,128)(2,1)} %copy.48) | copy-start | bytes 516100
  52.7 50.9 %copy-start.16 = (bf16[1,192,256]{2,1,0:T(8,128)(2,1)}, bf16[1,192,256]{2,1,0:T(8,128)(2,1)S(1)}, u32[]{:S(2)}) copy-start(bf16[1,192,256]{2,1,0:T(8,128)(2,1)S(1)} %all_gather.18) | copy-start | bytes 294916
  70.7 26.1 %copy-start.3 = (bf16[1,512,256]{2,1,0:T(8,128)(2,1)}, bf16[1,512,256]{2,1,0:T(8,128)(2,1)S(1)}, u32[]{:S(2)}) copy-start(bf16[1,512,256]{2,1,0:T(8,128)(2,1)S(1)} %all_gather.15) | copy-start | bytes 786436
  88.3 15.3 %copy-start.5 = (bf16[1,512,256]{2,1,0:T(8,128)(2,1)}, bf16[1,512,256]{2,1,0:T(8,128)(2,1)S(1)}, u32[]{:S(2)}) copy-start(bf16[1,512,256]{2,1,0:T(8,128)(2,1)S(1)} %all_gather.17) | copy-start | bytes 786436
  93.0 2.5 %copy-start.13 = (bf16[176,1,7,128]{3,2,1,0:T(8,128)(2,1)S(1)}, bf16[176,1,7,128]{3,2,1,0:T(8,128)(2,1)}, u32[]{:S(2)}) copy-start(bf16[176,1,7,128]{3,2,1,0:T(8,128)(2,1)} %get-tuple-element.30) | copy-start | bytes 946180
  101.1 3.7 %copy-start.11 = (bf16[176,1,7,128]{3,2,1,0:T(8,128)(2,1)S(1)}, bf16[176,1,7,128]{3,2,1,0:T(8,128)(2,1)}, u32[]{:S(2)}) copy-start(bf16[176,1,7,128]{3,2,1,0:T(8,128)(2,1)} %get-tuple-element.31) | copy-start | bytes 946180
  106.6 6.6 %copy-start.6 = (bf16[1,512,256]{2,1,0:T(8,128)(2,1)S(1)}, bf16[1,512,256]{2,1,0:T(8,128)(2,1)}, u32[]{:S(2)}) copy-start(bf16[1,512,256]{2,1,0:T(8,128)(2,1)} %copy-done.5) | copy-start | bytes 786436
  106.6 6.6 %copy-start.14 = (bf16[176,1,7,128]{3,2,1,0:T(8,128)(2,1)S(1)}, bf16[176,1,7,128]{3,2,1,0:T(8,128)(2,1)}, u32[]{:S(2)}) copy-start(bf16[176,1,7,128]{3,2,1,0:T(8,128)(2,1)} %get-tuple-element.30) | copy-start | bytes 946180
  106.7 6.6 %copy-start.30 = (f32[176,7]{0,1:T(8,128)S(1)}, f32[176,7]{0,1:T(8,128)}, u32[]{:S(2)}) copy-start(f32[176,7]{0,1:T(8,128)} %get-tuple-element.42) | copy-start | bytes 14788
  107.7 38.4 %all-to-all-start = ((bf16[176,8,4,56]{0,3,1,2:T(8,128)(2,1)}), bf16[176,8,4,56]{0,3,1,2:T(8,128)(2,1)S(1)}, u32[]{:S(2)}, u32[]{:S(2)}) async-start(bf16[176,8,4,56]{0,3,1,2:T(8,128)(2,1)} %copy.54), calls=%async_computation.1 | async-start | bytes 1835008 | tf_op jit(solution)/shard_map/all_to_all | solution.py:39
  113.2 47.2 %reduce-scatter.3.cloned.1.call-start = ((), (), s32[]{:S(2)}) async-start(), calls=%async_computation.3 | async-start | bytes 901120 | tf_op jit(solution)/shard_map/reduce_scatter | solution.py:196
  113.2 4.1 %copy-start.21 = (bf16[128,2,7,128]{3,0,2,1:T(8,128)(2,1)S(1)}, bf16[128,2,7,128]{3,0,2,1:T(8,128)(2,1)}, u32[]{:S(2)}) copy-start(bf16[128,2,7,128]{3,0,2,1:T(8,128)(2,1)} %copy-done.19) | copy-start | bytes 1376260
  113.2 4.1 %copy-start.25 = (bf16[48,2,7,128]{3,0,2,1:T(8,128)(2,1)S(1)}, bf16[48,2,7,128]{3,0,2,1:T(8,128)(2,1)}, u32[]{:S(2)}) copy-start(bf16[48,2,7,128]{3,0,2,1:T(8,128)(2,1)} %copy.48) | copy-start | bytes 516100
  117.3 1.5 copy-start.1
  117.3 1.6 copy-start.12
  118.1 2.2 %copy-start.2 = (f32[7,176,704]{2,1,0:T(8,128)S(1)}, f32[7,176,704]{2,1,0:T(8,128)}, u32[]{:S(2)}) copy-start(f32[7,176,704]{2,1,0:T(8,128)} %get-tuple-element.37) | copy-start | bytes 10407940
  118.1 2.2 %copy-start.17 = (bf16[1,192,256]{2,1,0:T(8,128)(2,1)S(1)}, bf16[1,192,256]{2,1,0:T(8,128)(2,1)}, u32[]{:S(2)}) copy-start(bf16[1,192,256]{2,1,0:T(8,128)(2,1)} %copy-done.16) | copy-start | bytes 294916
  118.1 2.2 %copy-start.29 = (f32[176,7]{0,1:T(8,128)S(1)}, f32[176,7]{0,1:T(8,128)}, u32[]{:S(2)}) copy-start(f32[176,7]{0,1:T(8,128)} %get-tuple-element.38) | copy-start | bytes 14788
  123.7 77.8 %reduce-scatter.5.cloned.1.call-start = ((), (), s32[]{:S(2)}) async-start(), calls=%async_computation.5 | async-start | bytes 3612672 | tf_op jit(solution)/shard_map/reduce_scatter | solution.py:45
  154.0 1.6 copy-start.8
  (6 other events, 7.8 us)
Sparse Core Ops, SparseCore 0:
  9.9 115.1 all-gather.1
  128.0 22.7 reduce-scatter.2
  154.2 47.1 reduce-scatter.4
where the time goes:
time: 210 us
  blocking collectives  66.6 us (32%)
  waiting for transfers between devices  61.1 us (29%)
  matrix products  34.1 us (16%)
  local copies, waits for them, and re-layouts  16.1 us (8%)
  between operations  14.2 us (7%)
  other arithmetic  12.2 us (6%)
  starting transfers between devices  5.63 us (3%)
    reduce_scatter x1, waiting for transfers between devices, weight_gradient(): lax.psum_scatter(partial_term.astype(jnp.bfloat16), 'leaf', scatter_dimen...  38.7 us
    all_to_all x1, waiting for transfers between devices, weight_gradient(): lax.all_to_all(parted, 'seq', split_axis=2, concat_axis=0, tiled=True)  22.3 us
    all_gather x1, blocking collectives, body(): lax.all_gather(prompt_k, 'seq', axis=1, tiled=True)  18.1 us
    all_gather x1, blocking collectives, body(): lax.all_gather(prompt_value_rows, 'seq', axis=1, tiled=True)  17.5 us
    all_gather x1, blocking collectives, body(): lax.all_gather(leaf_k, 'seq', axis=1, tiled=True)  16 us
    all_gather x1, blocking collectives, body(): lax.all_gather(leaf_value_rows, 'seq', axis=1, tiled=True)  15 us
    dot_general x1, matrix products, body(): lax.dot_general(upstream, out_weight, (((1,), (1,)), ((), ())), preferred...  9.1 us
    unnamed x70, local copies, waits for them, and re-layouts  7.78 us
  transfers between devices with their start and end apart: 4, of which 2 were waited for; matrix products, arithmetic and copies ran while one was open for 25% of the time, Pallas kernels for 0%

commit v1 on v0

--- a/solution.py
+++ b/solution.py
@@ -36,7 +36,15 @@
     row_share = width_total // (tree_count * seq_count)
     normalizer = 1.0 / math.sqrt(tree_count * seq_count * device_rows)
     parted = attn_out.reshape(device_rows, tree_count, seq_count, row_share)
-    moved = lax.all_to_all(parted, "seq", split_axis=2, concat_axis=0, tiled=True)
+    moved = jnp.concatenate(
+        jax.lax.all_to_all(
+            jnp.stack(jnp.split(parted, jax.lax.axis_size("seq"), axis=2), axis=0),
+            "seq",
+            split_axis=0,
+            concat_axis=0,
+        ),
+        axis=0,
+    )
     picked = moved.reshape(device_rows * seq_count, tree_count * row_share)
     tree_grad = lax.all_gather(upstream, "seq", axis=0, tiled=True)
     partial_term = lax.dot_general(

time: 210 us -> 210 us (level)
    unnamed x70 -> x76, local copies, waits for them, and re-layouts: 7.78 us -> 7.72 us
where the time goes in v1:
time: 210 us
  blocking collectives  66.2 us (32%)
  waiting for transfers between devices  61 us (29%)
  matrix products  34.7 us (17%)
  local copies, waits for them, and re-layouts  15 us (7%)
  between operations  14.3 us (7%)
  other arithmetic  13.3 us (6%)
  starting transfers between devices  5.52 us (3%)
    reduce_scatter x1, waiting for transfers between devices, weight_gradient(): lax.psum_scatter(partial_term.astype(jnp.bfloat16), 'leaf', scatter_dimen...  38.8 us
    all_to_all x1, waiting for transfers between devices, weight_gradient(): jax.lax.all_to_all(jnp.stack(jnp.split(parted, jax.lax.axis_size('seq'),...  22.1 us
    all_gather x1, blocking collectives, body(): lax.all_gather(prompt_k, 'seq', axis=1, tiled=True)  18.1 us
    all_gather x1, blocking collectives, body(): lax.all_gather(prompt_value_rows, 'seq', axis=1, tiled=True)  17.8 us
    all_gather x1, blocking collectives, body(): lax.all_gather(leaf_k, 'seq', axis=1, tiled=True)  16 us
    all_gather x1, blocking collectives, body(): lax.all_gather(leaf_value_rows, 'seq', axis=1, tiled=True)  14.4 us
    dot_general x1, matrix products, body(): lax.dot_general(upstream, out_weight, (((1,), (1,)), ((), ())), preferred...  8.98 us
    sub x2, matrix products, body(): shifted = jnp.exp(scores - jnp.max(scores, axis=2, keepdims=True))  7.74 us
  transfers between devices with their start and end apart: 4, of which 2 were waited for; matrix products, arithmetic and copies ran while one was open for 25% of the time, Pallas kernels for 0%

profile of v1, /device:TPU:0, one launch (start us, length us, event | category | flops | bytes accessed | tf_op | source)
XLA Modules:
  0.0 209.9 jit_solution(6407642861152149729)
XLA Ops:
  7.3 2.5 %pad_maximum_fusion = bf16[176,3584]{1,0:T(8,128)(2,1)} fusion(bf16[48,3584]{1,0:T(8,128)(2,1)} %bitcast.208, bf16[128,3584]{1,0:T(8,128)(2,1)} %bitcast.197), kind=kLoop, calls=%fused_computation.31 | loop fusion | flops 2523136 | bytes 2523136 | tf_op jit(solution)/shard_map/concatenate | solution.py:91
  11.5 1.0 copy.41
  12.5 9.0 %convolution_convert_fusion.1 = bf16[176,1792]{1,0:T(8,128)(2,1)S(1)} fusion(bf16[1792,3584]{1,0:T(8,128)(2,1)} %param.20, bf16[48,3584]{1,0:T(8,128)(2,1)S(1)} %bitcast.209, bf16[128,3584]{1,0:T(8,128)(2,1)S(1)} %bitcast.198), kind=kOutput, calls=%fused_computation.17 | convolution fusion | flops 2263568384 | bytes 14737408 | tf_op jit(solution)/shard_map/dot_general | solution.py:107
  22.3 16.0 %all_gather.16 = bf16[1,192,256]{2,1,0:T(8,128)(2,1)S(1)} all-gather(bf16[1,48,256]{2,1,0:T(8,128)(2,1)S(1)} %copy-done.30), channel_id=1, replica_groups=mesh['leaf'=8,'seq'=4] {'seq'}, dimensions={1}, use_global_device_ids=true | all-gather | bytes 122880 | tf_op jit(solution)/shard_map/all_gather | solution.py:85
  38.2 14.4 %all_gather.18 = bf16[1,192,256]{2,1,0:T(8,128)(2,1)S(1)} all-gather(bf16[1,48,256]{2,1,0:T(8,128)(2,1)S(1)} %copy-done.31), channel_id=1, replica_groups=mesh['leaf'=8,'seq'=4] {'seq'}, dimensions={1}, use_global_device_ids=true | all-gather | bytes 122880 | tf_op jit(solution)/shard_map/all_gather | solution.py:86
  52.7 18.1 %all_gather.15 = bf16[1,512,256]{2,1,0:T(8,128)(2,1)S(1)} all-gather(bf16[1,128,256]{2,1,0:T(8,128)(2,1)S(1)} %copy-done.28), channel_id=1, replica_groups=mesh['leaf'=8,'seq'=4] {'seq'}, dimensions={1}, use_global_device_ids=true | all-gather | bytes 327680 | tf_op jit(solution)/shard_map/all_gather | solution.py:83
  70.8 17.8 %all_gather.17 = bf16[1,512,256]{2,1,0:T(8,128)(2,1)S(1)} all-gather(bf16[1,128,256]{2,1,0:T(8,128)(2,1)S(1)} %copy-done.29), channel_id=1, replica_groups=mesh['leaf'=8,'seq'=4] {'seq'}, dimensions={1}, use_global_device_ids=true | all-gather | bytes 327680 | tf_op jit(solution)/shard_map/all_gather | solution.py:84
  89.0 3.3 %fusion.76 = (f32[7,176]{1,0:T(8,128)S(1)}, f32[7,176,704]{2,1,0:T(8,128)}) fusion(pred[176,704]{1,0:T(8,128)(4,1)S(1)} %pad_add_fusion, bf16[192,256]{1,0:T(8,128)(2,1)S(1)} %bitcast.199, bf16[512,256]{1,0:T(8,128)(2,1)S(1)} %bitcast.185, bf16[48,2,7,128]{3,0,2,1:T(8,128)(2,1)S(1)} %copy-done.24, bf16[128,2,7,128]{3,0,2,1:T(8,128)(2,1)S(1)} %copy-done.20), kind=kOutput, calls=%fused_computation.103 | convolution fusion | flops 226497216 | bytes 4589376 | tf_op jit(solution)/shard_map/sub | solution.py:125
  92.4 2.4 %fusion.17 = bf16[7,176,704]{2,1,0:T(8,128)(2,1)S(1)} fusion(f32[7,176,704]{2,1,0:T(8,128)} %get-tuple-element.38, f32[7,176]{1,0:T(8,128)S(1)} %get-tuple-element.37), kind=kLoop, calls=%fused_computation.27 | loop fusion | flops 1734656 | bytes 5208896 | tf_op jit(solution)/shard_map/convert_element_type | solution.py:127
  94.8 2.0 multiply_reduce_fusion
  96.8 4.4 %fusion.67 = (f32[7,176]{1,0:T(8,128)S(1)}, f32[7,176,704]{2,1,0:T(8,128)}) fusion(pred[176,704]{1,0:T(8,128)(4,1)} %copy-done.27, bf16[512,256]{1,0:T(8,128)(2,1)S(1)} %bitcast.186, bf16[192,256]{1,0:T(8,128)(2,1)S(1)} %bitcast.200, bf16[128,2,7,128]{3,0,2,1:T(8,128)(2,1)} %copy.41, bf16[48,2,7,128]{3,0,2,1:T(8,128)(2,1)S(1)} %copy-done.25), kind=kOutput, calls=%fused_computation.102 | convolution fusion | flops 226497216 | bytes 4589376 | tf_op jit(solution)/shard_map/sub | solution.py:125
  101.3 2.4 %fusion.16 = bf16[7,176,704]{2,1,0:T(8,128)(2,1)S(1)} fusion(f32[7,176,704]{2,1,0:T(8,128)} %get-tuple-element.34, f32[7,176]{1,0:T(8,128)S(1)} %get-tuple-element.33), kind=kLoop, calls=%fused_computation.26 | loop fusion | flops 1734656 | bytes 5208896 | tf_op jit(solution)/shard_map/convert_element_type | solution.py:127
  103.7 1.2 copy-done
  104.9 1.4 multiply_reduce_fusion.1
  106.8 1.1 pad_maximum_fusion.1
  107.9 5.4 %all-to-all-start = ((bf16[4,176,8,1,56]{1,4,2,3,0:T(8,128)(2,1)}), bf16[4,176,8,1,56]{1,4,2,3,0:T(8,128)(2,1)S(1)}, u32[]{:S(2)}, u32[]{:S(2)}) async-start(bf16[4,176,8,1,56]{1,4,2,3,0:T(8,128)(2,1)} %pad_maximum_fusion.1), calls=%async_computation.1 | async-start | bytes 1835008 | tf_op jit(solution)/shard_map/all_to_all | solution.py:40
  113.4 2.7 %fusion.4 = bf16[7,176,704]{2,1,0:T(8,128)(2,1)S(1)} fusion(f32[7,176]{1,0:T(8,128)S(1)} %bitcast.211, f32[7,176,704]{2,1,0:T(8,128)} %get-tuple-element.38, f32[7,176]{1,0:T(8,128)S(1)} %get-tuple-element.37, bf16[176,1,7,128]{3,2,1,0:T(8,128)(2,1)S(1)} %copy-done.14, bf16[192,256]{1,0:T(8,128)(2,1)} %bitcast.205, bf16[512,256]{1,0:T(8,128)(2,1)S(1)} %bitcast.191), kind=kOutput, calls=%fused_computation.6 | convolution fusion | flops 226733056 | bytes 5889664 | tf_op jit(solution)/shard_map/qhd,kd->hqk/dot_general | solution.py:145
  116.2 1.3 copy-done.7
  117.5 0.7 convolution_bitcast_fusion.4
  120.4 1.1 fusion.7
  121.5 0.7 convolution_bitcast_fusion.5
  122.8 0.9 pad_maximum_fusion.2
  123.8 22.1 %all-to-all-done = bf16[4,176,8,1,56]{1,4,2,3,0:T(8,128)(2,1)S(1)} async-done(((bf16[4,176,8,1,56]{1,4,2,3,0:T(8,128)(2,1)}), bf16[4,176,8,1,56]{1,4,2,3,0:T(8,128)(2,1)S(1)}, u32[]{:S(2)}, u32[]{:S(2)}) %all-to-all-start) | async-done | bytes 630816 | tf_op jit(solution)/shard_map/all_to_all | solution.py:40
  146.6 0.7 reshape_reshape.7
  147.4 6.5 %convolution_convert_fusion = bf16[448,3584]{1,0:T(8,128)(2,1)} fusion(bf16[704,448]{0,1:T(8,128)(2,1)S(1)} %reshape_reshape.7, bf16[704,3584]{1,0:T(8,128)(2,1)} %all-gather.2.cloned.1.call-done), kind=kOutput, calls=%fused_computation.2 | convolution fusion | flops 2262335488 | bytes 8888320 | tf_op jit(solution)/shard_map/dot_general | solution.py:50
  153.9 0.9 copy-done.4
  156.2 0.9 copy-done.10
  158.1 1.2 copy.52
  159.5 0.8 broadcast_in_dim.33
  160.3 1.0 convert_element_type.75
  162.6 38.8 %reduce-scatter.5.cloned.1.call-done = bf16[56,3584]{1,0:T(8,128)(2,1)} async-done(((bf16[448,3584]{1,0:T(8,128)(2,1)}), bf16[56,3584]{1,0:T(8,128)(2,1)}) %reduce-scatter.5.cloned.1.call-update) | async-done | bytes 401424 | tf_op jit(solution)/shard_map/reduce_scatter | solution.py:53
  201.5 1.9 convert_multiply_fusion
  (113 shorter events, 10.9 us)
Async XLA Ops:
  7.2 2.6 %copy-start.34 = (s32[1,16]{1,0:T(1,128)S(1)}, s32[1,16]{1,0:T(1,128)}, u32[]{:S(2)}) copy-start(s32[1,16]{1,0:T(1,128)} %param.21) | copy-start | bytes 196
  7.2 3.0 %copy-start.36 = (s32[1,16]{1,0:T(1,128)S(1)}, s32[1,16]{1,0:T(1,128)}, u32[]{:S(2)}) copy-start(s32[1,16]{1,0:T(1,128)} %param.23) | copy-start | bytes 196
  7.2 3.0 %copy-start.35 = (s32[1,16]{1,0:T(1,128)S(1)}, s32[1,16]{1,0:T(1,128)}, u32[]{:S(2)}) copy-start(s32[1,16]{1,0:T(1,128)} %param.22) | copy-start | bytes 196
  7.2 3.1 %copy-start.23 = (bf16[1,48,1792]{2,1,0:T(8,128)(2,1)S(1)}, bf16[1,48,1792]{2,1,0:T(8,128)(2,1)}, u32[]{:S(2)}) copy-start(bf16[1,48,1792]{2,1,0:T(8,128)(2,1)} %param.15) | copy-start | bytes 516100
  7.2 4.0 %copy-start.19 = (bf16[1,128,1792]{2,1,0:T(8,128)(2,1)S(1)}, bf16[1,128,1792]{2,1,0:T(8,128)(2,1)}, u32[]{:S(2)}) copy-start(bf16[1,128,1792]{2,1,0:T(8,128)(2,1)} %param.12) | copy-start | bytes 1376260
  7.2 140.2 %all-gather.2.cloned.1.call-start = ((), (), s32[]{:S(2)}) async-start(), calls=%async_computation.4 | async-start | bytes 6307840 | tf_op jit(solution)/shard_map/all_gather | solution.py:49
  9.8 2.7 %copy-start.16 = (bf16[1,128,3584]{2,1,0:T(8,128)(2,1)S(1)}, bf16[1,128,3584]{2,1,0:T(8,128)(2,1)}, u32[]{:S(2)}) copy-start(bf16[1,128,3584]{2,1,0:T(8,128)(2,1)} %param.18) | copy-start | bytes 2752516
  9.8 2.7 %copy-start.22 = (bf16[1,48,3584]{2,1,0:T(8,128)(2,1)S(1)}, bf16[1,48,3584]{2,1,0:T(8,128)(2,1)}, u32[]{:S(2)}) copy-start(bf16[1,48,3584]{2,1,0:T(8,128)(2,1)} %param.19) | copy-start | bytes 1032196
  12.5 9.8 %copy-start.30 = (bf16[1,48,256]{2,1,0:T(8,128)(2,1)S(1)}, bf16[1,48,256]{2,1,0:T(8,128)(2,1)}, u32[]{:S(2)}) copy-start(bf16[1,48,256]{2,1,0:T(8,128)(2,1)} %param.16) | copy-start | bytes 73732
  12.5 25.8 %copy-start.31 = (bf16[1,48,256]{2,1,0:T(8,128)(2,1)S(1)}, bf16[1,48,256]{2,1,0:T(8,128)(2,1)}, u32[]{:S(2)}) copy-start(bf16[1,48,256]{2,1,0:T(8,128)(2,1)} %param.17) | copy-start | bytes 73732
  12.5 40.2 %copy-start.28 = (bf16[1,128,256]{2,1,0:T(8,128)(2,1)S(1)}, bf16[1,128,256]{2,1,0:T(8,128)(2,1)}, u32[]{:S(2)}) copy-start(bf16[1,128,256]{2,1,0:T(8,128)(2,1)} %param.13) | copy-start | bytes 196612
  12.5 58.3 %copy-start.29 = (bf16[1,128,256]{2,1,0:T(8,128)(2,1)S(1)}, bf16[1,128,256]{2,1,0:T(8,128)(2,1)}, u32[]{:S(2)}) copy-start(bf16[1,128,256]{2,1,0:T(8,128)(2,1)} %param.14) | copy-start | bytes 196612
  21.5 67.5 %copy-start.20 = (bf16[128,2,7,128]{3,0,2,1:T(8,128)(2,1)S(1)}, bf16[128,2,7,128]{3,0,2,1:T(8,128)(2,1)}, u32[]{:S(2)}) copy-start(bf16[128,2,7,128]{3,0,2,1:T(8,128)(2,1)} %copy.41) | copy-start | bytes 1376260
  21.5 67.5 %copy-start.24 = (bf16[48,2,7,128]{3,0,2,1:T(8,128)(2,1)S(1)}, bf16[48,2,7,128]{3,0,2,1:T(8,128)(2,1)}, u32[]{:S(2)}) copy-start(bf16[48,2,7,128]{3,0,2,1:T(8,128)(2,1)} %copy.42) | copy-start | bytes 516100
  52.7 51.0 %copy-start.17 = (bf16[1,192,256]{2,1,0:T(8,128)(2,1)}, bf16[1,192,256]{2,1,0:T(8,128)(2,1)S(1)}, u32[]{:S(2)}) copy-start(bf16[1,192,256]{2,1,0:T(8,128)(2,1)S(1)} %all_gather.18) | copy-start | bytes 294916
  70.8 26.1 %copy-start.3 = (bf16[1,512,256]{2,1,0:T(8,128)(2,1)}, bf16[1,512,256]{2,1,0:T(8,128)(2,1)S(1)}, u32[]{:S(2)}) copy-start(bf16[1,512,256]{2,1,0:T(8,128)(2,1)S(1)} %all_gather.15) | copy-start | bytes 786436
  88.5 15.1 %copy-start.5 = (bf16[1,512,256]{2,1,0:T(8,128)(2,1)}, bf16[1,512,256]{2,1,0:T(8,128)(2,1)S(1)}, u32[]{:S(2)}) copy-start(bf16[1,512,256]{2,1,0:T(8,128)(2,1)S(1)} %all_gather.17) | copy-start | bytes 786436
  88.9 3.4 %copy-start.27 = (pred[176,704]{1,0:T(8,128)(4,1)}, pred[176,704]{1,0:T(8,128)(4,1)S(1)}, u32[]{:S(2)}) copy-start(pred[176,704]{1,0:T(8,128)(4,1)S(1)} %pad_add_fusion) | copy-start | bytes 371716
  89.0 5.8 %copy-start.13 = (bf16[176,1,7,128]{3,2,1,0:T(8,128)(2,1)}, bf16[176,1,7,128]{3,2,1,0:T(8,128)(2,1)S(1)}, u32[]{:S(2)}) copy-start(bf16[176,1,7,128]{3,2,1,0:T(8,128)(2,1)S(1)} %get-tuple-element.27) | copy-start | bytes 946180
  89.0 14.7 %copy-start.11 = (bf16[176,1,7,128]{3,2,1,0:T(8,128)(2,1)}, bf16[176,1,7,128]{3,2,1,0:T(8,128)(2,1)S(1)}, u32[]{:S(2)}) copy-start(bf16[176,1,7,128]{3,2,1,0:T(8,128)(2,1)S(1)} %get-tuple-element.28) | copy-start | bytes 946180
  103.6 2.7 %copy-start.15 = (bf16[128,7,176]{0,2,1:T(8,128)(2,1)S(1)}, bf16[128,7,176]{0,2,1:T(8,128)(2,1)}, u32[]{:S(2)}) copy-start(bf16[128,7,176]{0,2,1:T(8,128)(2,1)} %get-tuple-element.40) | copy-start | bytes 946180
  106.7 6.7 %copy-start.6 = (bf16[1,512,256]{2,1,0:T(8,128)(2,1)S(1)}, bf16[1,512,256]{2,1,0:T(8,128)(2,1)}, u32[]{:S(2)}) copy-start(bf16[1,512,256]{2,1,0:T(8,128)(2,1)} %copy-done.5) | copy-start | bytes 786436
  106.7 6.7 %copy-start.14 = (bf16[176,1,7,128]{3,2,1,0:T(8,128)(2,1)S(1)}, bf16[176,1,7,128]{3,2,1,0:T(8,128)(2,1)}, u32[]{:S(2)}) copy-start(bf16[176,1,7,128]{3,2,1,0:T(8,128)(2,1)} %copy-done.13) | copy-start | bytes 946180
  106.7 6.7 %copy-start.33 = (f32[176,7]{0,1:T(8,128)S(1)}, f32[176,7]{0,1:T(8,128)}, u32[]{:S(2)}) copy-start(f32[176,7]{0,1:T(8,128)} %get-tuple-element.39) | copy-start | bytes 14788
  107.9 38.0 %all-to-all-start = ((bf16[4,176,8,1,56]{1,4,2,3,0:T(8,128)(2,1)}), bf16[4,176,8,1,56]{1,4,2,3,0:T(8,128)(2,1)S(1)}, u32[]{:S(2)}, u32[]{:S(2)}) async-start(bf16[4,176,8,1,56]{1,4,2,3,0:T(8,128)(2,1)} %pad_maximum_fusion.1), calls=%async_computation.1 | async-start | bytes 1835008 | tf_op jit(solution)/shard_map/all_to_all | solution.py:40
  113.4 46.9 %reduce-scatter.3.cloned.1.call-start = ((), (), s32[]{:S(2)}) async-start(), calls=%async_computation.3 | async-start | bytes 901120 | tf_op jit(solution)/shard_map/reduce_scatter | solution.py:204
  113.4 4.1 %copy-start.21 = (bf16[128,2,7,128]{3,0,2,1:T(8,128)(2,1)S(1)}, bf16[128,2,7,128]{3,0,2,1:T(8,128)(2,1)}, u32[]{:S(2)}) copy-start(bf16[128,2,7,128]{3,0,2,1:T(8,128)(2,1)} %copy.41) | copy-start | bytes 1376260
  113.4 4.0 %copy-start.26 = (bf16[48,2,7,128]{3,0,2,1:T(8,128)(2,1)S(1)}, bf16[48,2,7,128]{3,0,2,1:T(8,128)(2,1)}, u32[]{:S(2)}) copy-start(bf16[48,2,7,128]{3,0,2,1:T(8,128)(2,1)} %copy.42) | copy-start | bytes 516100
  118.2 2.2 %copy-start.2 = (f32[7,176,704]{2,1,0:T(8,128)S(1)}, f32[7,176,704]{2,1,0:T(8,128)}, u32[]{:S(2)}) copy-start(f32[7,176,704]{2,1,0:T(8,128)} %get-tuple-element.34) | copy-start | bytes 10407940
  118.2 2.2 %copy-start.18 = (bf16[1,192,256]{2,1,0:T(8,128)(2,1)S(1)}, bf16[1,192,256]{2,1,0:T(8,128)(2,1)}, u32[]{:S(2)}) copy-start(bf16[1,192,256]{2,1,0:T(8,128)(2,1)} %copy-done.17) | copy-start | bytes 294916
  118.2 2.2 %copy-start.32 = (f32[176,7]{0,1:T(8,128)S(1)}, f32[176,7]{0,1:T(8,128)}, u32[]{:S(2)}) copy-start(f32[176,7]{0,1:T(8,128)} %get-tuple-element.35) | copy-start | bytes 14788
  123.8 77.7 %reduce-scatter.5.cloned.1.call-start = ((), (), s32[]{:S(2)}) async-start(), calls=%async_computation.5 | async-start | bytes 3612672 | tf_op jit(solution)/shard_map/reduce_scatter | solution.py:53
  (9 other events, 13.0 us)
Sparse Core Ops, SparseCore 0:
  9.9 114.9 all-gather.1
  127.8 22.9 reduce-scatter.2
  154.2 47.2 reduce-scatter.4
